TPU v7x, 512 devices: a whole 4x8x8 slice. The times are simulated.
512 devices in a mesh: group: 8 (over z), shard: 16 (over y, x_lo), tensor: 4 (over x_hi, core).
Axes of the slice: x: 4 (x_hi: 2, x_lo: 2; x = x_hi * 2 + x_lo), y: 8, z: 8, core: 2. Of those that a mesh axis runs over, the one named last changes fastest.
Arguments:
- attn_in_local: bfloat16 [8, 768, 2304], P('group', 'shard', 'tensor'), may hold values from -6 to 6
- attn_out_local: bfloat16 [8, 768, 768], P('group', 'shard', 'tensor'), may hold values from -6 to 6
- ffn_in_local: bfloat16 [8, 768, 3072], P('group', 'shard', 'tensor'), may hold values from -6 to 6
- ffn_out_local: bfloat16 [8, 3072, 768], P('group', 'shard', 'tensor'), may hold values from -6 to 6
- small_local: bfloat16 [8, 1920], P('group'), may hold values from -6 to 6
- dense_old: float32 [64, 110592], P(('shard', 'tensor'), 'group'), may hold values from -6 to 6
- dense_momentum: float32 [64, 110592], P(('shard', 'tensor'), 'group'), may hold values from -6 to 6
- small_old: float32 [1920], P('group'), may hold values from -6 to 6
- small_momentum: float32 [1920], P('group'), may hold values from -6 to 6
- embed_local: bfloat16 [8, 768, 8192], P('group', 'shard', 'tensor'), may hold values from -6 to 6
- embed_old: float32 [768, 8192], P('shard', 'tensor'), may hold values from -6 to 6
- basis: float32 [768, 64], P('shard'), may hold values from -0.21875 to 0.21875
- coeff_momentum: float32 [64, 8192], P(None, 'tensor'), may hold values from -6 to 6
Outputs:
- attn_in_next: float32 [768, 2304], P('shard', 'tensor')
- attn_out_next: float32 [768, 768], P('shard', 'tensor')
- ffn_in_next: float32 [768, 3072], P('shard', 'tensor')
- ffn_out_next: float32 [3072, 768], P('shard', 'tensor')
- dense_momentum_next: float32 [64, 110592], P(('shard', 'tensor'), 'group')
- small_next: float32 [1920], replicated
- small_momentum_next: float32 [1920], P('group')
- embed_next: float32 [768, 8192], P('shard', 'tensor')
- coeff_momentum_next: float32 [64, 8192], P(None, 'tensor')
All inputs are finite; a program needn't handle non-finite values.
Results may differ from a plain program's by a relative error of at most 0.0003.
Values sent between devices are 32-bit elements; how exact they have to be, the bound alone decides.
A program may use at most 64 MiB of HBM per device.

v0:
```python
import jax
import jax.numpy as jnp
from jax import lax
from jax.sharding import PartitionSpec as P

momentum_coef = 0.5
outer_rate = 0.7


def nesterov(old_value, momentum, delta):
    moved = momentum_coef * momentum + delta
    return (old_value - outer_rate * (delta + momentum_coef * moved), moved)


def shards(
    attn_in_local,
    attn_out_local,
    ffn_in_local,
    ffn_out_local,
    small_local,
    dense_old,
    dense_momentum,
    small_old,
    small_momentum,
    embed_local,
    embed_old,
    basis,
    coeff_momentum,
):
    groups = lax.axis_size("group")
    matrices = (attn_in_local, attn_out_local, ffn_in_local, ffn_out_local)
    local_terms = jnp.concatenate([matrix[0].reshape(-1) for matrix in matrices]).astype(
        jnp.float32
    )
    small_terms = small_local[0].astype(jnp.float32)
    old_flat = dense_old[0]
    momentum_flat = dense_momentum[0]
    dense_part, small_part = (
        lax.psum_scatter(local_terms, "group", scatter_dimension=0, tiled=True),
        lax.psum_scatter(small_terms, "group", scatter_dimension=0, tiled=True),
    )
    dense_new, dense_moved = nesterov(old_flat, momentum_flat, old_flat - dense_part / groups)
    small_new, small_moved = nesterov(small_old, small_momentum, small_old - small_part / groups)
    full_flat, small_next = (
        lax.all_gather(dense_new, "group", axis=0, tiled=True),
        lax.all_gather(small_new, "group", axis=0, tiled=True),
    )
    results = []
    offset = 0
    for matrix in matrices:
        block_size = matrix.shape[1] * matrix.shape[2]
        results.append(
            full_flat[offset : offset + block_size].reshape(matrix.shape[1], matrix.shape[2])
        )
        offset = offset + block_size
    difference = embed_old - embed_local[0].astype(jnp.float32)
    partial_coeff = lax.dot_general(
        basis,
        difference,
        (((0,), (0,)), ((), ())),
        precision=lax.Precision.HIGHEST,
        preferred_element_type=jnp.float32,
    )
    coeff = lax.psum(partial_coeff, ("group", "shard")) / groups
    coeff_moved = momentum_coef * coeff_momentum + coeff
    update = coeff + momentum_coef * coeff_moved
    embed_next = embed_old - outer_rate * jnp.dot(
        basis, update, precision=lax.Precision.HIGHEST, preferred_element_type=jnp.float32
    )
    return (
        results[0],
        results[1],
        results[2],
        results[3],
        dense_moved[None, :],
        small_next,
        small_moved,
        embed_next,
        coeff_moved,
    )


def solution(mesh):
    placed = (
        P("group", "shard", "tensor"),
        P("group", "shard", "tensor"),
        P("group", "shard", "tensor"),
        P("group", "shard", "tensor"),
        P("group", None),
        P(("shard", "tensor"), "group"),
        P(("shard", "tensor"), "group"),
        P("group"),
        P("group"),
        P("group", "shard", "tensor"),
        P("shard", "tensor"),
        P("shard", None),
        P(None, "tensor"),
    )
    return jax.shard_map(
        shards,
        mesh=mesh,
        in_specs=placed,
        out_specs=(
            P("shard", "tensor"),
            P("shard", "tensor"),
            P("shard", "tensor"),
            P("shard", "tensor"),
            P(("shard", "tensor"), "group"),
            P(),
            P("group"),
            P("shard", "tensor"),
            P(None, "tensor"),
        ),
        check_vma=False,
    )
```

profile of v0, /device:TPU:6, one launch (start us, length us, event | category | flops | bytes accessed | tf_op | source)
XLA Modules:
  0.0 1209.7 jit_solution(16336643338121977493)
XLA Ops:
  7.2 0.8 reshape_squeeze.13
  8.1 1.0 reshape_squeeze.12
  9.2 0.8 copy-done.6
  10.1 0.8 maximum_convert_fusion
  11.2 0.6 copy-done.5
  11.9 1.4 convolution_bitcast_fusion
  13.3 0.6 copy-done.13
  14.0 0.6 fusion.15
  15.9 23.5 %all-reduce.2 = f32[1920]{0:T(1024)S(1)} all-reduce(f32[1920]{0:T(1024)S(1)} %convert_reduce_fusion), channel_id=3, replica_groups=mesh['group'=8,'shard'=16,'tensor'=4] {'group'}, use_global_device_ids=true, to_apply=%region_1.0.clone | all-reduce | flops 1920 | bytes 15360
  40.1 0.6 copy-done.11
  40.8 0.6 subtract_dynamic-update-slice_fusion
  41.4 14.9 %all-reduce = f32[1920]{0:T(1024)} all-reduce(f32[1920]{0:T(1024)S(1)} %get-tuple-element.9), channel_id=1, replica_groups=mesh['group'=8,'shard'=16,'tensor'=4] {'group'}, use_global_device_ids=true, to_apply=%add | all-reduce | flops 1920 | bytes 15360
  56.5 0.7 copy-done.9
  57.3 38.3 %all-reduce.8.cloned.1.call-done = f32[110592]{0:T(1024)} async-done(((f32[110592]{0:T(1024)}), f32[110592]{0:T(1024)}) %all-reduce.8.cloned.1.call-update) | async-done | bytes 442384
  95.6 0.9 multiply_subtract_fusion
  96.6 25.3 %all-gather = f32[8,1,13824]{2,1,0:T(1,128)S(1)} all-gather(f32[1,1,13824]{2,1,0:T(1,128)S(1)} %reshape.74), channel_id=1, replica_groups=mesh['group'=8,'shard'=16,'tensor'=4] {'group'}, dimensions={0}, use_global_device_ids=true | all-gather | bytes 497664 | tf_op jit(solution)/shard_map/all_gather | solution.py:45
  121.9 0.7 broadcast_in_dim.3
  122.6 0.7 reshape.67
  123.6 0.8 reshape.66
  124.4 0.8 reshape.68
  125.1 0.7 slice.49
  125.8 1074.4 %all-reduce.6.cloned.1.call-done = f32[64,2048]{1,0:T(8,128)} async-done(((f32[64,2048]{1,0:T(8,128)}), f32[64,2048]{1,0:T(8,128)}) %all-reduce.6.cloned.1.call-update) | async-done | bytes 524304 | tf_op jit(solution)/shard_map/psum | solution.py:64
  1200.2 1.2 multiply_add_fusion
  1201.5 1.3 fusion.1
  (37 shorter events, 1.4 us)
Async XLA Ops:
  7.2 3.8 copy-start
  7.2 1.9 copy-start.7
  7.2 88.4 %all-reduce.8.cloned.1.call-start = ((), (), s32[]{:S(2)}) async-start(), calls=%async_computation.1 | async-start | bytes 884736
  9.1 0.9 copy-start.6
  10.1 1.1 copy-start.3
  10.9 1.0 copy-start.5
  10.9 1189.3 %all-reduce.6.cloned.1.call-start = ((), (), s32[]{:S(2)}) async-start(), calls=%async_computation | async-start | bytes 1048576 | tf_op jit(solution)/shard_map/psum | solution.py:64
  13.3 0.7 copy-start.13
  13.3 2.6 copy-start.10
  13.3 43.1 %copy-start.8 = (f32[1,13824]{1,0:T(1,128)S(1)}, f32[1,13824]{1,0:T(1,128)}, u32[]{:S(2)}) copy-start(f32[1,13824]{1,0:T(1,128)} %param.19) | copy-start | bytes 165892
  40.1 0.7 copy-start.11
  40.1 0.7 copy-start.12
  56.4 0.8 copy-start.9
  123.3 1077.0 %copy-start.4 = (f32[64,2048]{1,0:T(8,128)S(1)}, f32[64,2048]{1,0:T(8,128)}, u32[]{:S(2)}) copy-start(f32[64,2048]{1,0:T(8,128)} %param.25) | copy-start | bytes 1572868
  1200.2 1.2 copy-start.1
  1201.5 1.3 copy-start.2
Sparse Core Ops, SparseCore 0:
  11.1 84.5 all-reduce.7
  99.1 1101.0 all-reduce.5
where the time goes:
time: 1210 us
  waiting for transfers between devices  1110 us (92%)
  blocking collectives  63.8 us (5%)
  between operations  16.2 us (1%)
    psum x1, waiting for transfers between devices, shards(): coeff = lax.psum(partial_coeff, ('group', 'shard')) / groups  1070 us
    unnamed x2, blocking collectives  38.5 us
    unnamed x3, waiting for transfers between devices  38.3 us
    all_gather x1, blocking collectives, shards(): lax.all_gather(dense_new, 'group', axis=0, tiled=True)  25.3 us
  transfers between devices with their start and end apart: 2, of which 2 were waited for; matrix products, arithmetic and copies ran while one was open for 1% of the time, Pallas kernels for 0%

commit v1 on v0

v1 whole, which is shorter than its diff:
```python
import functools

import jax
import jax.numpy as jnp
from jax import lax
from jax.experimental import pallas as pl
from jax.experimental.pallas import tpu as pltpu
from jax.sharding import PartitionSpec as P

momentum_coef = 0.5
outer_rate = 0.7

MESH = pl.DeviceIdType.MESH
F32 = jnp.float32
BF16 = jnp.bfloat16

NZ = 8
NY = 8
NX = 2
ROWS = 112
DENSE_ROWS = 108
RANK = 64
Q = 2

PLAN = (
    (0, 0, 0, 24, 0),
    (0, 1, 24, 24, 0),
    (1, 2, 0, 48, 0),
    (2, 2, 0, 6, 72),
    (2, 3, 6, 18, 0),
    (2, 4, 24, 18, 0),
    (2, 5, 42, 6, 0),
    (3, 5, 0, 48, 36),
    (3, 6, 48, 72, 0),
    (3, 7, 120, 72, 0),
)
WIDTHS = (576, 192, 768, 192)
HEIGHTS = (48, 48, 48, 192)
TILES = tuple(-(-width // 128) for width in WIDTHS)


def nesterov(old_value, momentum, delta):
    moved = momentum_coef * momentum + delta
    return (old_value - outer_rate * (delta + momentum_coef * moved), moved)


def lower_lanes(shape):
    return lax.broadcasted_iota(jnp.int32, shape, 1) < 64


def pack(tiles, flat):
    for which, owner, row, count, base in PLAN:
        xs = tiles[which]
        full = WIDTHS[which] // 128
        if WIDTHS[which] % 128 == 0:
            for t in range(full):
                flat[owner, pl.ds(base + t, count, stride=full), :] = xs[t, pl.ds(row, count), :]
            continue
        n, step = count // 2, 2 * full + 1
        low = lower_lanes((n, 128))
        even = [xs[t, pl.ds(row, n, stride=2), :] for t in range(full + 1)]
        turned = [
            pltpu.roll(xs[t, pl.ds(row + 1, n, stride=2), :], 64, 1) for t in range(full + 1)
        ]
        for t in range(full):
            flat[owner, pl.ds(base + t, n, stride=step), :] = even[t]
        flat[owner, pl.ds(base + full, n, stride=step), :] = jnp.where(low, even[full], turned[0])
        for t in range(full):
            flat[owner, pl.ds(base + full + 1 + t, n, stride=step), :] = jnp.where(
                low, turned[t], turned[t + 1]
            )


def unpack(flat, tiles):
    for which, owner, row, count, base in PLAN:
        xs = tiles[which]
        full = WIDTHS[which] // 128
        if WIDTHS[which] % 128 == 0:
            for t in range(full):
                xs[t, pl.ds(row, count), :] = flat[owner, pl.ds(base + t, count, stride=full), :]
            continue
        n, step = count // 2, 2 * full + 1
        low = lower_lanes((n, 128))
        rows = [flat[owner, pl.ds(base + t, n, stride=step), :] for t in range(step)]
        for t in range(full + 1):
            xs[t, pl.ds(row, n, stride=2), :] = rows[t]
        for t in range(full):
            xs[t, pl.ds(row + 1, n, stride=2), :] = pltpu.roll(
                jnp.where(low, rows[full + 1 + t], rows[full + t]), 64, 1
            )
        xs[full, pl.ds(row + 1, n, stride=2), :] = pltpu.roll(rows[2 * full], 64, 1)


def split_bf16(value):
    high = value.astype(BF16)
    return high, (value - high.astype(F32)).astype(BF16)


def flows(n):
    long, short = n // 2, n - 1 - n // 2
    order = []
    for q in range(Q):
        order += [(0, q, 1, long), (1, q, -1, long)]
    for q in range(Q):
        order += [(1, q, 1, short), (0, q, -1, short)]
    return order


def comm_kernel(*refs):
    (ai, ao, fi, fo, sl, dold, dmom, sold, smom, el, eo, ba) = refs[:12]
    full_out, moved_out, cfull_out = refs[12:15]
    (
        ai_v, ao_v, fi_v, fo_v, sl_v, dold_v, dmom_v, sold_v, smom_v, el_v, eo_v, ba_v,
        ai_x, ao_x, fi_x, fo_x, old_x, mom_x,
        dpart, dslots, dfull, dmoved,
        cpart, cslots, cmine, cmid, ctile, cfull,
        load_sem, store_sem,
        zs_sem, zr_sem, zas_sem, zar_sem,
        ys_sem, yr_sem, yas_sem, yar_sem,
        ms_sem, mr_sem, mas_sem, mar_sem,
    ) = refs[15:]

    z = lax.axis_index("group")
    shard = lax.axis_index("shard")
    y = shard // NX
    x = lax.rem(shard, NX)

    def at_z(offset):
        return {"group": lax.rem(z + offset + NZ, NZ)}

    def at_y(offset):
        return {"shard": lax.rem(y + offset + NY, NY) * NX + x}

    def at_mid(dx, dz):
        return {"group": lax.rem(z + dz, NZ), "shard": y * NX + lax.rem(x + dx, NX)}

    peers = [(dx, dz) for dx in range(NX) for dz in range(NZ) if dx or dz]

    loads = []
    for i, (src, dst) in enumerate(
        (
            (el, el_v), (eo, eo_v), (ba, ba_v), (ai, ai_v), (ao, ao_v), (fi, fi_v), (fo, fo_v),
            (sl, sl_v), (dold, dold_v), (dmom, dmom_v), (sold, sold_v), (smom, smom_v),
        )
    ):
        copy = pltpu.make_async_copy(src, dst, load_sem.at[i])
        copy.start()
        loads.append(copy)

    barrier = pltpu.get_barrier_semaphore()
    greeted = [at_y(1), at_y(-1)] + [at_mid(dx, dz) for dx, dz in peers]
    for peer in greeted:
        pl.semaphore_signal(barrier, inc=1, device_id=peer, device_id_type=MESH)

    for copy in loads[:3]:
        copy.wait()
    b_high, b_low = split_bf16(ba_v[...])
    left = jnp.concatenate([b_high, b_low, b_high, b_low], axis=0)

    for t in range(NY):
        c = lax.rem(y + 4 + t, NY)
        columns = pl.ds(pl.multiple_of(c * 256, 256), 256)
        high, low = split_bf16(eo_v[:, columns] - el_v[0, :, columns].astype(F32))
        right = jnp.concatenate([high, high, low, low], axis=0)
        product = lax.dot_general(
            left, right, (((0,), (0,)), ((), ())), preferred_element_type=F32
        )
        cpart[c, 0] = product[:, :128].reshape(NZ, 8, 128)
        cpart[c, 1] = product[:, 128:].reshape(NZ, 8, 128)

    pl.semaphore_wait(barrier, len(greeted))

    zflows, yflows = flows(NZ), flows(NY)
    zcuts = {}
    for half in range(2):
        bounds = (0, 32, 56) if Q == 2 else (0, 56)
        for q in range(Q):
            zcuts[half, q] = (half * 56 + bounds[q], bounds[q + 1] - bounds[q])

    def zpiece(ref, lead, half, q):
        start, size = zcuts[half, q]
        return ref.at[lead, pl.ds(start, size)]

    def ypiece(ref, lead, half, q):
        return ref.at[lead, half, pl.ds(q * (NZ // Q), NZ // Q)]

    sends = []

    def send(src, dst, send_sem, recv_sem, device):
        copy = pltpu.make_async_remote_copy(
            src_ref=src, dst_ref=dst, send_sem=send_sem, recv_sem=recv_sem,
            device_id=device, device_id_type=MESH,
        )
        copy.start()
        sends.append(copy)
        return copy

    def slot_of(f, s):
        return f * 4 + s

    rs_copies = {}

    def rs_send(axis, f, s):
        if axis == "z":
            half, q, way, hops = zflows[f]
            piece, part, slots, me, n, target = zpiece, dpart, dslots, z, NZ, at_z(way)
            ss, rr = zs_sem, zr_sem
        else:
            half, q, way, hops = yflows[f]
            piece, part, slots, me, n, target = ypiece, cpart, cslots, y, NY, at_y(way)
            ss, rr = ys_sem, yr_sem
        lead = 7 if way > 0 else 3
        del lead
        if s == 0:
            src = piece(part, lax.rem(me + way * hops + n, n), half, q)
        else:
            src = slot_ref(axis, f, s - 1)
        rs_copies[axis, f, s] = send(
            src, slot_ref(axis, f, s), ss.at[slot_of(f, s)], rr.at[slot_of(f, s)], target
        )

    def slot_ref(axis, f, s):
        half, q, way, hops = (zflows if axis == "z" else yflows)[f]
        lead = (0 if way > 0 else 4) + s
        if axis == "z":
            return zpiece(dslots, lead, half, q)
        return ypiece(cslots, lead, half, q)

    def rs_step(axis, f, s):
        half, q, way, hops = (zflows if axis == "z" else yflows)[f]
        rs_copies[axis, f, s].wait_recv()
        if s == hops - 1:
            return
        slot = slot_ref(axis, f, s)
        if axis == "z":
            own = zpiece(dpart, lax.rem(z + way * (hops - s - 1) + NZ, NZ), half, q)
        else:
            own = ypiece(cpart, lax.rem(y + way * (hops - s - 1) + NY, NY), half, q)
        slot[...] = slot[...] + own[...]
        rs_send(axis, f, s + 1)

    for f in range(len(yflows)):
        rs_send("y", f, 0)

    for copy in loads[3:]:
        copy.wait()
    for which, (src, dst) in enumerate(
        ((ai_v, ai_x), (ao_v, ao_x), (fi_v, fi_x), (fo_v, fo_x))
    ):
        for t in range(TILES[which]):
            size = min(128, WIDTHS[which] - 128 * t)
            dst[t, :, 0:size] = src[0, :, 128 * t : 128 * t + size].astype(F32)
    pack((ai_x, ao_x, fi_x, fo_x), dpart)
    small = sl_v[...].astype(F32)
    for owner in range(NZ):
        dpart[owner, 104:112, :] = jnp.where(
            lax.broadcasted_iota(jnp.int32, (8, 128), 0) < 4, dpart[owner, 104:112, :], 0.0
        )
        dpart[owner, 108:109, :] = small[:, 240 * owner : 240 * owner + 128]
        dpart[owner, 109:110, 0:112] = small[:, 240 * owner + 128 : 240 * owner + 240]

    for f in range(len(zflows)):
        rs_send("z", f, 0)

    for src, dst, small_src in ((dold_v, old_x, sold_v), (dmom_v, mom_x, smom_v)):
        dst[104:112, :] = jnp.zeros((8, 128), F32)
        for r in range(DENSE_ROWS):
            dst[r : r + 1, :] = src[:, 128 * r : 128 * r + 128]
        dst[108:109, :] = small_src[:, 0:128]
        dst[109:110, 0:112] = small_src[:, 128:240]

    for s in range(NZ // 2):
        for f in range(len(yflows)):
            if s < yflows[f][3]:
                rs_step("y", f, s)
        for f in range(len(zflows)):
            if s < zflows[f][3]:
                rs_step("z", f, s)

    long_y, short_y = NY // 2, NY - 1 - NY // 2
    cmine[0] = cpart[y, 0] + cslots[long_y - 1, 0] + cslots[4 + short_y - 1, 0]
    cmine[1] = cpart[y, 1] + cslots[short_y - 1, 1] + cslots[4 + long_y - 1, 1]
    mid = []
    for k, (dx, dz) in enumerate(peers):
        mid.append(
            send(
                cmine.at[lax.rem(x + dx, NX), lax.rem(z + dz, NZ)], cmid.at[k],
                ms_sem.at[k], mr_sem.at[k], at_mid(dx, dz),
            )
        )

    long_z, short_z = NZ // 2, NZ - 1 - NZ // 2
    for half, (right, left_) in enumerate(((long_z, short_z), (short_z, long_z))):
        rows = slice(56 * half, 56 * half + 56)
        total = dpart[z, rows] + dslots[right - 1, rows] + dslots[4 + left_ - 1, rows]
        old = old_x[rows, :]
        new, moved = nesterov(old, mom_x[rows, :], old - total / NZ)
        dfull[z, rows] = new
        dmoved[rows, :] = moved

    ag_copies = {}

    def ag_send(axis, f, s):
        half, q, way, hops = (zflows if axis == "z" else yflows)[f]
        if axis == "z":
            ref = zpiece(dfull, lax.rem(z - way * s + NZ, NZ), half, q)
            ss, rr, target = zas_sem, zar_sem, at_z(way)
        else:
            ref = ypiece(cfull, lax.rem(y - way * s + NY, NY), half, q)
            ss, rr, target = yas_sem, yar_sem, at_y(way)
        ag_copies[axis, f, s] = send(
            ref, ref, ss.at[slot_of(f, s)], rr.at[slot_of(f, s)], target
        )

    def ag_step(axis, f, s):
        hops = (zflows if axis == "z" else yflows)[f][3]
        ag_copies[axis, f, s].wait_recv()
        if s < hops - 1:
            ag_send(axis, f, s + 1)

    for f in range(len(zflows)):
        ag_send("z", f, 0)

    tile = cmine[x, z]
    for k in range(len(peers)):
        mid[k].wait_recv()
        tile = tile + cmid[k]
    ctile[...] = tile
    cfull[y, x, z] = tile
    mid_back = []
    for k, (dx, dz) in enumerate(peers):
        mid_back.append(
            send(ctile, cfull.at[y, x, z], mas_sem.at[k], mar_sem.at[k], at_mid(dx, dz))
        )

    for s in range(NZ // 2):
        for f in range(len(zflows)):
            if s < zflows[f][3]:
                ag_step("z", f, s)

    for copy in mid_back:
        copy.wait_recv()
    for f in range(len(yflows)):
        ag_send("y", f, 0)

    stores = [
        pltpu.make_async_copy(dfull, full_out, store_sem.at[0]),
        pltpu.make_async_copy(dmoved, moved_out, store_sem.at[1]),
    ]
    for copy in stores:
        copy.start()
    for s in range(NY // 2):
        for f in range(len(yflows)):
            if s < yflows[f][3]:
                ag_step("y", f, s)
    for copy in sends:
        copy.wait_send()
    last = pltpu.make_async_copy(cfull, cfull_out, store_sem.at[2])
    last.start()
    for copy in stores:
        copy.wait()
    last.wait()


def finish_kernel(
    full, moved, cfull, eo, ba, cm,
    ai_o, ao_o, fi_o, fo_o, dm_o, sn_o, sm_o, en_o, cm_o,
    ai_x, ao_x, fi_x, fo_x,
):
    b_high, b_low = split_bf16(ba[...])
    left = jnp.concatenate([b_high, b_low, b_high, b_low], axis=1)
    for c in range(NY):
        for j in range(2):
            columns = slice(256 * c + 128 * j, 256 * c + 128 * j + 128)
            coeff = cfull[c, j].reshape(RANK, 128) / NZ
            coeff_moved = momentum_coef * cm[:, columns] + coeff
            cm_o[:, columns] = coeff_moved
            high, low = split_bf16(coeff + momentum_coef * coeff_moved)
            right = jnp.concatenate([high, high, low, low], axis=0)
            product = jnp.dot(left, right, preferred_element_type=F32)
            en_o[:, columns] = eo[:, columns] - outer_rate * product
    unpack(full, (ai_x, ao_x, fi_x, fo_x))
    for which, (src, dst) in enumerate(((ai_x, ai_o), (ao_x, ao_o), (fi_x, fi_o), (fo_x, fo_o))):
        for t in range(TILES[which]):
            size = min(128, WIDTHS[which] - 128 * t)
            dst[:, 128 * t : 128 * t + size] = src[t, :, 0:size]
    for r in range(DENSE_ROWS):
        dm_o[:, 128 * r : 128 * r + 128] = moved[r : r + 1, :]
    sm_o[:, 0:128] = moved[108:109, :]
    sm_o[:, 128:240] = moved[109:110, 0:112]
    for owner in range(NZ):
        sn_o[:, 240 * owner : 240 * owner + 128] = full[owner, 108:109, :]
        sn_o[:, 240 * owner + 128 : 240 * owner + 240] = full[owner, 109:110, 0:112]


def shards(
    attn_in_local,
    attn_out_local,
    ffn_in_local,
    ffn_out_local,
    small_local,
    dense_old,
    dense_momentum,
    small_old,
    small_momentum,
    embed_local,
    embed_old,
    basis,
    coeff_momentum,
):
    any_spec = pl.BlockSpec(memory_space=pl.ANY)
    vmem_spec = pl.BlockSpec(memory_space=pltpu.VMEM)
    dma = pltpu.SemaphoreType.DMA
    tile_scratch = [
        pltpu.VMEM((TILES[i], HEIGHTS[i], 128), F32) for i in range(4)
    ]
    operands = (
        attn_in_local, attn_out_local, ffn_in_local, ffn_out_local, small_local,
        dense_old, dense_momentum, small_old[None, :], small_momentum[None, :],
        embed_local, embed_old, basis,
    )
    nflows = 4 * Q
    full, moved, cfull = pl.pallas_call(
        comm_kernel,
        out_shape=(
            jax.ShapeDtypeStruct((NZ, ROWS, 128), F32),
            jax.ShapeDtypeStruct((ROWS, 128), F32),
            jax.ShapeDtypeStruct((NY, NX, NZ, 8, 128), F32),
        ),
        in_specs=[any_spec] * len(operands),
        out_specs=[any_spec] * 3,
        scratch_shapes=[pltpu.VMEM(a.shape, a.dtype) for a in operands]
        + tile_scratch
        + [
            pltpu.VMEM((ROWS, 128), F32),
            pltpu.VMEM((ROWS, 128), F32),
            pltpu.VMEM((NZ, ROWS, 128), F32),
            pltpu.VMEM((8, ROWS, 128), F32),
            pltpu.VMEM((NZ, ROWS, 128), F32),
            pltpu.VMEM((ROWS, 128), F32),
            pltpu.VMEM((NY, NX, NZ, 8, 128), F32),
            pltpu.VMEM((8, NX, NZ, 8, 128), F32),
            pltpu.VMEM((NX, NZ, 8, 128), F32),
            pltpu.VMEM((NX * NZ - 1, 8, 128), F32),
            pltpu.VMEM((8, 128), F32),
            pltpu.VMEM((NY, NX, NZ, 8, 128), F32),
            dma((len(operands),)),
            dma((3,)),
        ]
        + [dma((nflows * 4,))] * 8
        + [dma((NX * NZ - 1,))] * 4,
        compiler_params=pltpu.CompilerParams(collective_id=0, has_side_effects=True),
        name="exchange",
    )(*operands)

    outs = pl.pallas_call(
        finish_kernel,
        out_shape=(
            jax.ShapeDtypeStruct((48, 576), F32),
            jax.ShapeDtypeStruct((48, 192), F32),
            jax.ShapeDtypeStruct((48, 768), F32),
            jax.ShapeDtypeStruct((192, 192), F32),
            jax.ShapeDtypeStruct((1, 13824), F32),
            jax.ShapeDtypeStruct((1, 1920), F32),
            jax.ShapeDtypeStruct((1, 240), F32),
            jax.ShapeDtypeStruct((48, 2048), F32),
            jax.ShapeDtypeStruct((RANK, 2048), F32),
        ),
        in_specs=[vmem_spec] * 6,
        out_specs=[vmem_spec] * 9,
        scratch_shapes=tile_scratch,
        name="finish",
    )(full, moved, cfull, embed_old, basis, coeff_momentum)
    return (
        outs[0], outs[1], outs[2], outs[3], outs[4],
        outs[5].reshape(-1), outs[6].reshape(-1), outs[7], outs[8],
    )


def solution(mesh):
    placed = (
        P("group", "shard", "tensor"),
        P("group", "shard", "tensor"),
        P("group", "shard", "tensor"),
        P("group", "shard", "tensor"),
        P("group", None),
        P(("shard", "tensor"), "group"),
        P(("shard", "tensor"), "group"),
        P("group"),
        P("group"),
        P("group", "shard", "tensor"),
        P("shard", "tensor"),
        P("shard", None),
        P(None, "tensor"),
    )
    return jax.shard_map(
        shards,
        mesh=mesh,
        in_specs=placed,
        out_specs=(
            P("shard", "tensor"),
            P("shard", "tensor"),
            P("shard", "tensor"),
            P("shard", "tensor"),
            P(("shard", "tensor"), "group"),
            P(),
            P("group"),
            P("shard", "tensor"),
            P(None, "tensor"),
        ),
        check_vma=False,
    )
```

time: 1210 us -> 66.1 us (0.05)
  waiting for transfers between devices: 1110 us -> 0 us
  Pallas kernels: 0 us -> 63.9 us
  blocking collectives: 63.8 us -> 0 us
  between operations: 16.2 us -> 0.66 us
    psum x1 -> x0, waiting for transfers between devices: 1070 us -> none  [shards(): coeff = lax.psum(partial_coeff, ('group', 'shard')) / groups]
    pallas_call x0 -> x2, Pallas kernels: none -> 63.9 us  [the longest x1 61 us: shards(): pl.pallas_call(comm_kernel, out_shape=(jax.ShapeDtypeStruct((NZ, ROWS, 12...]
    unnamed x2 -> x0, blocking collectives: 38.5 us -> none
    unnamed x3 -> x0, waiting for transfers between devices: 38.3 us -> none
    all_gather x1 -> x0, blocking collectives: 25.3 us -> none  [shards(): lax.all_gather(dense_new, 'group', axis=0, tiled=True)]
  transfers between devices with their start and end apart: 2 -> 0, of which waited for: 2 -> 0; matrix products, arithmetic and copies ran while one was open for 1% -> 0% of each run, Pallas kernels for 0% -> 0%
where the time goes in v1:
time: 66.1 us; the launch traced here: 65.8 us
  Pallas kernels  63.9 us (97%)
  local copies, waits for them, and re-layouts  0.7 us (1%)
    pallas_call x1, Pallas kernels, shards(): pl.pallas_call(comm_kernel, out_shape=(jax.ShapeDtypeStruct((NZ, ROWS, 12...  61 us
    pallas_call x1, Pallas kernels, shards(): pl.pallas_call(finish_kernel, out_shape=(jax.ShapeDtypeStruct((48, 576),...  2.91 us

profile of v1, /device:TPU:6, one launch (start us, length us, event | category | flops | bytes accessed | tf_op | source)
XLA Modules:
  0.0 65.8 jit_solution(14436808621721964821)
XLA Ops:
  0.6 61.0 %exchange.1 = (f32[8,112,128]{2,1,0:T(8,128)}, f32[112,128]{1,0:T(8,128)}, f32[8,2,8,8,128]{4,3,2,1,0:T(8,128)}) custom-call(bf16[1,48,576]{2,1,0:T(8,128)(2,1)} %refs_0_.1, bf16[1,48,192]{2,1,0:T(8,128)(2,1)} %refs_1_.1, bf16[1,48,768]{2,1,0:T(8,128)(2,1)} %refs_2_.1, bf16[1,192,192]{2,1,0:T(8,128)(2,1)} %refs_3_.1, bf16[1,1920]{1,0:T(2,128)(2,1)} %refs_4_.1, ...), custom_call_target="tpu_custom_call" | custom-call | tf_op jit(solution)/shard_map/exchange/pallas_call | solution.py:423
  61.6 2.9 %finish.1 = (f32[48,576]{1,0:T(8,128)}, f32[48,192]{1,0:T(8,128)}, f32[48,768]{1,0:T(8,128)}, f32[192,192]{1,0:T(8,128)}, f32[1,13824]{1,0:T(1,128)}, /*index=5*...) custom-call(f32[8,112,128]{2,1,0:T(8,128)} %get-tuple-element.21.full, ...), custom_call_target="tpu_custom_call" | custom-call | tf_op jit(solution)/shard_map/finish/pallas_call | solution.py:456
  64.5 0.0 copy-start
  64.5 0.7 %copy-done = f32[1,1920]{1,0:T(1,128)S(1)} copy-done((f32[1,1920]{1,0:T(1,128)S(1)}, f32[1,1920]{1,0:T(1,128)}, u32[]{:S(2)}) %copy-start) | copy-done | bytes 7704
  65.2 0.6 reduce
Async XLA Ops:
  64.5 0.7 %copy-start = (f32[1,1920]{1,0:T(1,128)S(1)}, f32[1,1920]{1,0:T(1,128)}, u32[]{:S(2)}) copy-start(f32[1,1920]{1,0:T(1,128)} %get-tuple-element.29) | copy-start | bytes 23044

commit v2 on v1

--- a/solution.py
+++ b/solution.py
@@ -20,7 +20,7 @@
 ROWS = 112
 DENSE_ROWS = 108
 RANK = 64
-Q = 2
+FAR_FIRST = (4, 3, -3, 2, -2, 1, -1)
 
 PLAN = (
     (0, 0, 0, 24, 0),
@@ -96,16 +96,6 @@
     return high, (value - high.astype(F32)).astype(BF16)
 
 
-def flows(n):
-    long, short = n // 2, n - 1 - n // 2
-    order = []
-    for q in range(Q):
-        order += [(0, q, 1, long), (1, q, -1, long)]
-    for q in range(Q):
-        order += [(1, q, 1, short), (0, q, -1, short)]
-    return order
-
-
 def comm_kernel(*refs):
     (ai, ao, fi, fo, sl, dold, dmom, sold, smom, el, eo, ba) = refs[:12]
     full_out, moved_out, cfull_out = refs[12:15]
@@ -132,9 +122,9 @@
         return {"shard": lax.rem(y + offset + NY, NY) * NX + x}
 
     def at_mid(dx, dz):
-        return {"group": lax.rem(z + dz, NZ), "shard": y * NX + lax.rem(x + dx, NX)}
-
-    peers = [(dx, dz) for dx in range(NX) for dz in range(NZ) if dx or dz]
+        return {"group": lax.rem(z + dz + NZ, NZ), "shard": y * NX + lax.rem(x + dx, NX)}
+
+    peers = [(dx, dz) for dz in FAR_FIRST for dx in (1, 0)] + [(1, 0)]
 
     loads = []
     for i, (src, dst) in enumerate(
@@ -148,17 +138,29 @@
         loads.append(copy)
 
     barrier = pltpu.get_barrier_semaphore()
-    greeted = [at_y(1), at_y(-1)] + [at_mid(dx, dz) for dx, dz in peers]
+    greeted = [at_y(offset) for offset in FAR_FIRST] + [at_mid(dx, dz) for dx, dz in peers]
     for peer in greeted:
         pl.semaphore_signal(barrier, inc=1, device_id=peer, device_id_type=MESH)
+
+    sends = []
+
+    def send(src, dst, send_sem, recv_sem, device):
+        copy = pltpu.make_async_remote_copy(
+            src_ref=src, dst_ref=dst, send_sem=send_sem, recv_sem=recv_sem,
+            device_id=device, device_id_type=MESH,
+        )
+        copy.start()
+        sends.append(copy)
+        return copy
 
     for copy in loads[:3]:
         copy.wait()
     b_high, b_low = split_bf16(ba_v[...])
     left = jnp.concatenate([b_high, b_low, b_high, b_low], axis=0)
 
-    for t in range(NY):
-        c = lax.rem(y + 4 + t, NY)
+    y_rs = []
+    for k, offset in enumerate(FAR_FIRST + (0,)):
+        c = lax.rem(y + offset + NY, NY)
         columns = pl.ds(pl.multiple_of(c * 256, 256), 256)
         high, low = split_bf16(eo_v[:, columns] - el_v[0, :, columns].astype(F32))
         right = jnp.concatenate([high, high, low, low], axis=0)
@@ -167,80 +169,12 @@
         )
         cpart[c, 0] = product[:, :128].reshape(NZ, 8, 128)
         cpart[c, 1] = product[:, 128:].reshape(NZ, 8, 128)
-
-    pl.semaphore_wait(barrier, len(greeted))
-
-    zflows, yflows = flows(NZ), flows(NY)
-    zcuts = {}
-    for half in range(2):
-        bounds = (0, 32, 56) if Q == 2 else (0, 56)
-        for q in range(Q):
-            zcuts[half, q] = (half * 56 + bounds[q], bounds[q + 1] - bounds[q])
-
-    def zpiece(ref, lead, half, q):
-        start, size = zcuts[half, q]
-        return ref.at[lead, pl.ds(start, size)]
-
-    def ypiece(ref, lead, half, q):
-        return ref.at[lead, half, pl.ds(q * (NZ // Q), NZ // Q)]
-
-    sends = []
-
-    def send(src, dst, send_sem, recv_sem, device):
-        copy = pltpu.make_async_remote_copy(
-            src_ref=src, dst_ref=dst, send_sem=send_sem, recv_sem=recv_sem,
-            device_id=device, device_id_type=MESH,
-        )
-        copy.start()
-        sends.append(copy)
-        return copy
-
-    def slot_of(f, s):
-        return f * 4 + s
-
-    rs_copies = {}
-
-    def rs_send(axis, f, s):
-        if axis == "z":
-            half, q, way, hops = zflows[f]
-            piece, part, slots, me, n, target = zpiece, dpart, dslots, z, NZ, at_z(way)
-            ss, rr = zs_sem, zr_sem
-        else:
-            half, q, way, hops = yflows[f]
-            piece, part, slots, me, n, target = ypiece, cpart, cslots, y, NY, at_y(way)
-            ss, rr = ys_sem, yr_sem
-        lead = 7 if way > 0 else 3
-        del lead
-        if s == 0:
-            src = piece(part, lax.rem(me + way * hops + n, n), half, q)
-        else:
-            src = slot_ref(axis, f, s - 1)
-        rs_copies[axis, f, s] = send(
-            src, slot_ref(axis, f, s), ss.at[slot_of(f, s)], rr.at[slot_of(f, s)], target
-        )
-
-    def slot_ref(axis, f, s):
-        half, q, way, hops = (zflows if axis == "z" else yflows)[f]
-        lead = (0 if way > 0 else 4) + s
-        if axis == "z":
-            return zpiece(dslots, lead, half, q)
-        return ypiece(cslots, lead, half, q)
-
-    def rs_step(axis, f, s):
-        half, q, way, hops = (zflows if axis == "z" else yflows)[f]
-        rs_copies[axis, f, s].wait_recv()
-        if s == hops - 1:
-            return
-        slot = slot_ref(axis, f, s)
-        if axis == "z":
-            own = zpiece(dpart, lax.rem(z + way * (hops - s - 1) + NZ, NZ), half, q)
-        else:
-            own = ypiece(cpart, lax.rem(y + way * (hops - s - 1) + NY, NY), half, q)
-        slot[...] = slot[...] + own[...]
-        rs_send(axis, f, s + 1)
-
-    for f in range(len(yflows)):
-        rs_send("y", f, 0)
+        if k == 0:
+            pl.semaphore_wait(barrier, len(greeted))
+        if offset:
+            y_rs.append(
+                send(cpart.at[c], cslots.at[k], ys_sem.at[k], yr_sem.at[k], at_y(offset))
+            )
 
     for copy in loads[3:]:
         copy.wait()
@@ -259,8 +193,10 @@
         dpart[owner, 108:109, :] = small[:, 240 * owner : 240 * owner + 128]
         dpart[owner, 109:110, 0:112] = small[:, 240 * owner + 128 : 240 * owner + 240]
 
-    for f in range(len(zflows)):
-        rs_send("z", f, 0)
+    z_rs = []
+    for k, offset in enumerate(FAR_FIRST):
+        src = dpart.at[lax.rem(z + offset + NZ, NZ)]
+        z_rs.append(send(src, dslots.at[k], zs_sem.at[k], zr_sem.at[k], at_z(offset)))
 
     for src, dst, small_src in ((dold_v, old_x, sold_v), (dmom_v, mom_x, smom_v)):
         dst[104:112, :] = jnp.zeros((8, 128), F32)
@@ -269,61 +205,45 @@
         dst[108:109, :] = small_src[:, 0:128]
         dst[109:110, 0:112] = small_src[:, 128:240]
 
-    for s in range(NZ // 2):
-        for f in range(len(yflows)):
-            if s < yflows[f][3]:
-                rs_step("y", f, s)
-        for f in range(len(zflows)):
-            if s < zflows[f][3]:
-                rs_step("z", f, s)
-
-    long_y, short_y = NY // 2, NY - 1 - NY // 2
-    cmine[0] = cpart[y, 0] + cslots[long_y - 1, 0] + cslots[4 + short_y - 1, 0]
-    cmine[1] = cpart[y, 1] + cslots[short_y - 1, 1] + cslots[4 + long_y - 1, 1]
+    for copy in y_rs:
+        copy.wait_recv()
+    for j in range(NX):
+        total = cpart[y, j]
+        for k in range(len(y_rs)):
+            total = total + cslots[k, j]
+        cmine[j] = total
     mid = []
     for k, (dx, dz) in enumerate(peers):
         mid.append(
             send(
-                cmine.at[lax.rem(x + dx, NX), lax.rem(z + dz, NZ)], cmid.at[k],
+                cmine.at[lax.rem(x + dx, NX), lax.rem(z + dz + NZ, NZ)], cmid.at[k],
                 ms_sem.at[k], mr_sem.at[k], at_mid(dx, dz),
             )
         )
 
-    long_z, short_z = NZ // 2, NZ - 1 - NZ // 2
-    for half, (right, left_) in enumerate(((long_z, short_z), (short_z, long_z))):
-        rows = slice(56 * half, 56 * half + 56)
-        total = dpart[z, rows] + dslots[right - 1, rows] + dslots[4 + left_ - 1, rows]
-        old = old_x[rows, :]
-        new, moved = nesterov(old, mom_x[rows, :], old - total / NZ)
-        dfull[z, rows] = new
-        dmoved[rows, :] = moved
-
-    ag_copies = {}
-
-    def ag_send(axis, f, s):
-        half, q, way, hops = (zflows if axis == "z" else yflows)[f]
-        if axis == "z":
-            ref = zpiece(dfull, lax.rem(z - way * s + NZ, NZ), half, q)
-            ss, rr, target = zas_sem, zar_sem, at_z(way)
-        else:
-            ref = ypiece(cfull, lax.rem(y - way * s + NY, NY), half, q)
-            ss, rr, target = yas_sem, yar_sem, at_y(way)
-        ag_copies[axis, f, s] = send(
-            ref, ref, ss.at[slot_of(f, s)], rr.at[slot_of(f, s)], target
-        )
-
-    def ag_step(axis, f, s):
-        hops = (zflows if axis == "z" else yflows)[f][3]
-        ag_copies[axis, f, s].wait_recv()
-        if s < hops - 1:
-            ag_send(axis, f, s + 1)
-
-    for f in range(len(zflows)):
-        ag_send("z", f, 0)
-
+    for copy in z_rs:
+        copy.wait_recv()
+    total = dpart[z]
+    for k in range(len(z_rs)):
+        total = total + dslots[k]
+    old = old_x[...]
+    new, moved = nesterov(old, mom_x[...], old - total / NZ)
+    dfull[z] = new
+    dmoved[...] = moved
+
+    z_ag = {}
+
+    def dense_send(k, offset):
+        z_ag[k] = send(dfull.at[z], dfull.at[z], zas_sem.at[k], zar_sem.at[k], at_z(offset))
+
+    for k, offset in enumerate(FAR_FIRST):
+        if abs(offset) < 3:
+            dense_send(k, offset)
+
+    for copy in mid:
+        copy.wait_recv()
     tile = cmine[x, z]
     for k in range(len(peers)):
-        mid[k].wait_recv()
         tile = tile + cmid[k]
     ctile[...] = tile
     cfull[y, x, z] = tile
@@ -332,40 +252,42 @@
         mid_back.append(
             send(ctile, cfull.at[y, x, z], mas_sem.at[k], mar_sem.at[k], at_mid(dx, dz))
         )
-
-    for s in range(NZ // 2):
-        for f in range(len(zflows)):
-            if s < zflows[f][3]:
-                ag_step("z", f, s)
+    for k, offset in enumerate(FAR_FIRST):
+        if abs(offset) >= 3:
+            dense_send(k, offset)
 
     for copy in mid_back:
         copy.wait_recv()
-    for f in range(len(yflows)):
-        ag_send("y", f, 0)
-
-    stores = [
-        pltpu.make_async_copy(dfull, full_out, store_sem.at[0]),
-        pltpu.make_async_copy(dmoved, moved_out, store_sem.at[1]),
-    ]
-    for copy in stores:
+    y_ag = []
+    for k, offset in enumerate(FAR_FIRST):
+        y_ag.append(send(cfull.at[y], cfull.at[y], yas_sem.at[k], yar_sem.at[k], at_y(offset)))
+
+    stores = [pltpu.make_async_copy(dmoved, moved_out, store_sem.at[0])]
+    stores[0].start()
+    copy = pltpu.make_async_copy(cfull.at[y], cfull_out.at[y], store_sem.at[2])
+    copy.start()
+    stores.append(copy)
+    for k in range(len(FAR_FIRST)):
+        z_ag[k].wait_recv()
+    copy = pltpu.make_async_copy(dfull, full_out, store_sem.at[1])
+    copy.start()
+    stores.append(copy)
+    for k in (5, 6, 3, 4, 1, 2, 0):
+        y_ag[k].wait_recv()
+        c = lax.rem(y - FAR_FIRST[k] + NY, NY)
+        copy = pltpu.make_async_copy(cfull.at[c], cfull_out.at[c], store_sem.at[3 + k])
         copy.start()
-    for s in range(NY // 2):
-        for f in range(len(yflows)):
-            if s < yflows[f][3]:
-                ag_step("y", f, s)
+        stores.append(copy)
     for copy in sends:
         copy.wait_send()
-    last = pltpu.make_async_copy(cfull, cfull_out, store_sem.at[2])
-    last.start()
     for copy in stores:
         copy.wait()
-    last.wait()
 
 
 def finish_kernel(
     full, moved, cfull, eo, ba, cm,
     ai_o, ao_o, fi_o, fo_o, dm_o, sn_o, sm_o, en_o, cm_o,
-    ai_x, ao_x, fi_x, fo_x,
+    ai_x, ao_x, fi_x, fo_x, sn_x,
 ):
     b_high, b_low = split_bf16(ba[...])
     left = jnp.concatenate([b_high, b_low, b_high, b_low], axis=1)
@@ -389,8 +311,10 @@
     sm_o[:, 0:128] = moved[108:109, :]
     sm_o[:, 128:240] = moved[109:110, 0:112]
     for owner in range(NZ):
-        sn_o[:, 240 * owner : 240 * owner + 128] = full[owner, 108:109, :]
-        sn_o[:, 240 * owner + 128 : 240 * owner + 240] = full[owner, 109:110, 0:112]
+        sn_x[:, 240 * owner : 240 * owner + 128] = full[owner, 108:109, :]
+        sn_x[:, 240 * owner + 128 : 240 * owner + 240] = full[owner, 109:110, 0:112]
+    for r in range(15):
+        sn_o[r : r + 1, :] = sn_x[:, 128 * r : 128 * r + 128]
 
 
 def shards(
@@ -419,7 +343,6 @@
         dense_old, dense_momentum, small_old[None, :], small_momentum[None, :],
         embed_local, embed_old, basis,
     )
-    nflows = 4 * Q
     full, moved, cfull = pl.pallas_call(
         comm_kernel,
         out_shape=(
@@ -435,19 +358,19 @@
             pltpu.VMEM((ROWS, 128), F32),
             pltpu.VMEM((ROWS, 128), F32),
             pltpu.VMEM((NZ, ROWS, 128), F32),
-            pltpu.VMEM((8, ROWS, 128), F32),
+            pltpu.VMEM((NZ - 1, ROWS, 128), F32),
             pltpu.VMEM((NZ, ROWS, 128), F32),
             pltpu.VMEM((ROWS, 128), F32),
             pltpu.VMEM((NY, NX, NZ, 8, 128), F32),
-            pltpu.VMEM((8, NX, NZ, 8, 128), F32),
+            pltpu.VMEM((NY - 1, NX, NZ, 8, 128), F32),
             pltpu.VMEM((NX, NZ, 8, 128), F32),
             pltpu.VMEM((NX * NZ - 1, 8, 128), F32),
             pltpu.VMEM((8, 128), F32),
             pltpu.VMEM((NY, NX, NZ, 8, 128), F32),
             dma((len(operands),)),
-            dma((3,)),
+            dma((10,)),
         ]
-        + [dma((nflows * 4,))] * 8
+        + [dma((7,))] * 8
         + [dma((NX * NZ - 1,))] * 4,
         compiler_params=pltpu.CompilerParams(collective_id=0, has_side_effects=True),
         name="exchange",
@@ -461,14 +384,14 @@
             jax.ShapeDtypeStruct((48, 768), F32),
             jax.ShapeDtypeStruct((192, 192), F32),
             jax.ShapeDtypeStruct((1, 13824), F32),
-            jax.ShapeDtypeStruct((1, 1920), F32),
+            jax.ShapeDtypeStruct((15, 128), F32),
             jax.ShapeDtypeStruct((1, 240), F32),
             jax.ShapeDtypeStruct((48, 2048), F32),
             jax.ShapeDtypeStruct((RANK, 2048), F32),
         ),
         in_specs=[vmem_spec] * 6,
         out_specs=[vmem_spec] * 9,
-        scratch_shapes=tile_scratch,
+        scratch_shapes=tile_scratch + [pltpu.VMEM((1, 1920), F32)],
         name="finish",
     )(full, moved, cfull, embed_old, basis, coeff_momentum)
     return (

time: 66.1 us -> 55.4 us (0.84)
  Pallas kernels: 63.9 us -> 54.1 us
  local copies, waits for them, and re-layouts: 0.7 us -> 0 us
    pallas_call x1, Pallas kernels: 61 us -> 51.2 us  [shards(): pl.pallas_call(comm_kernel, out_shape=(jax.ShapeDtypeStruct((NZ, ROWS, 12...]
    unnamed x2 -> x0, local copies, waits for them, and re-layouts: 0.7 us -> none
where the time goes in v2:
time: 55.4 us; the launch traced here: 54.7 us
  Pallas kernels  54.1 us (98%)
  between operations  0.65 us (1%)
    pallas_call x1, Pallas kernels, shards(): pl.pallas_call(comm_kernel, out_shape=(jax.ShapeDtypeStruct((NZ, ROWS, 12...  51.2 us
    pallas_call x1, Pallas kernels, shards(): pl.pallas_call(finish_kernel, out_shape=(jax.ShapeDtypeStruct((48, 576),...  2.92 us

profile of v2, /device:TPU:6, one launch (start us, length us, event | category | flops | bytes accessed | tf_op | source)
XLA Modules:
  0.0 54.7 jit_solution(10697328473902060319)
XLA Ops:
  0.6 51.2 %exchange.1 = (f32[8,112,128]{2,1,0:T(8,128)}, f32[112,128]{1,0:T(8,128)}, f32[8,2,8,8,128]{4,3,2,1,0:T(8,128)}) custom-call(bf16[1,48,576]{2,1,0:T(8,128)(2,1)} %refs_0_.1, bf16[1,48,192]{2,1,0:T(8,128)(2,1)} %refs_1_.1, bf16[1,48,768]{2,1,0:T(8,128)(2,1)} %refs_2_.1, bf16[1,192,192]{2,1,0:T(8,128)(2,1)} %refs_3_.1, bf16[1,1920]{1,0:T(2,128)(2,1)} %refs_4_.1, ...), custom_call_target="tpu_custom_call" | custom-call | tf_op jit(solution)/shard_map/exchange/pallas_call | solution.py:346
  51.8 2.9 %finish.1 = (f32[48,576]{1,0:T(8,128)}, f32[48,192]{1,0:T(8,128)}, f32[48,768]{1,0:T(8,128)}, f32[192,192]{1,0:T(8,128)}, f32[1,13824]{1,0:T(1,128)}, /*index=5*...) custom-call(f32[8,112,128]{2,1,0:T(8,128)} %get-tuple-element.21.full, ...), custom_call_target="tpu_custom_call" | custom-call | tf_op jit(solution)/shard_map/finish/pallas_call | solution.py:379

commit v3 on v2

--- a/solution.py
+++ b/solution.py
@@ -21,6 +21,9 @@
 DENSE_ROWS = 108
 RANK = 64
 FAR_FIRST = (4, 3, -3, 2, -2, 1, -1)
+NEAR = (3, 4, 5, 6)
+VIA_IN = ()
+VIA_OUT = (4, 3, -3, 2, -2)
 
 PLAN = (
     (0, 0, 0, 24, 0),
@@ -103,7 +106,7 @@
         ai_v, ao_v, fi_v, fo_v, sl_v, dold_v, dmom_v, sold_v, smom_v, el_v, eo_v, ba_v,
         ai_x, ao_x, fi_x, fo_x, old_x, mom_x,
         dpart, dslots, dfull, dmoved,
-        cpart, cslots, cmine, cmid, ctile, cfull,
+        cpart, cslots, xslots, cmine, ctiles, cfull,
         load_sem, store_sem,
         zs_sem, zr_sem, zas_sem, zar_sem,
         ys_sem, yr_sem, yas_sem, yar_sem,
@@ -118,13 +121,10 @@
     def at_z(offset):
         return {"group": lax.rem(z + offset + NZ, NZ)}
 
-    def at_y(offset):
-        return {"shard": lax.rem(y + offset + NY, NY) * NX + x}
-
-    def at_mid(dx, dz):
-        return {"group": lax.rem(z + dz + NZ, NZ), "shard": y * NX + lax.rem(x + dx, NX)}
-
-    peers = [(dx, dz) for dz in FAR_FIRST for dx in (1, 0)] + [(1, 0)]
+    def at_yx(dy, dx):
+        return {"shard": lax.rem(y + dy + NY, NY) * NX + lax.rem(x + dx, NX)}
+
+    peers = [(dy, dx) for dy in FAR_FIRST for dx in (1, 0)] + [(0, 1)]
 
     loads = []
     for i, (src, dst) in enumerate(
@@ -138,7 +138,7 @@
         loads.append(copy)
 
     barrier = pltpu.get_barrier_semaphore()
-    greeted = [at_y(offset) for offset in FAR_FIRST] + [at_mid(dx, dz) for dx, dz in peers]
+    greeted = [at_yx(dy, dx) for dy, dx in peers] + [at_z(offset) for offset in FAR_FIRST]
     for peer in greeted:
         pl.semaphore_signal(barrier, inc=1, device_id=peer, device_id_type=MESH)
 
@@ -158,8 +158,8 @@
     b_high, b_low = split_bf16(ba_v[...])
     left = jnp.concatenate([b_high, b_low, b_high, b_low], axis=0)
 
-    y_rs = []
-    for k, offset in enumerate(FAR_FIRST + (0,)):
+    rs, halves = [], {}
+    for offset in FAR_FIRST + (0,):
         c = lax.rem(y + offset + NY, NY)
         columns = pl.ds(pl.multiple_of(c * 256, 256), 256)
         high, low = split_bf16(eo_v[:, columns] - el_v[0, :, columns].astype(F32))
@@ -169,12 +169,18 @@
         )
         cpart[c, 0] = product[:, :128].reshape(NZ, 8, 128)
         cpart[c, 1] = product[:, 128:].reshape(NZ, 8, 128)
-        if k == 0:
+        if offset == FAR_FIRST[0]:
             pl.semaphore_wait(barrier, len(greeted))
-        if offset:
-            y_rs.append(
-                send(cpart.at[c], cslots.at[k], ys_sem.at[k], yr_sem.at[k], at_y(offset))
-            )
+        for k, (dy, dx) in enumerate(peers):
+            if dy == offset and dy in VIA_IN:
+                if dx:
+                    halves[dy] = send(
+                        cpart.at[c, 1 - x], xslots.at[VIA_IN.index(dy)],
+                        ys_sem.at[k], yr_sem.at[k], at_yx(0, 1),
+                    )
+            elif dy == offset:
+                src = cpart.at[c, lax.rem(x + dx, NX)]
+                rs.append(send(src, cslots.at[k], ys_sem.at[k], yr_sem.at[k], at_yx(dy, dx)))
 
     for copy in loads[3:]:
         copy.wait()
@@ -198,6 +204,15 @@
         src = dpart.at[lax.rem(z + offset + NZ, NZ)]
         z_rs.append(send(src, dslots.at[k], zs_sem.at[k], zr_sem.at[k], at_z(offset)))
 
+    for k, (dy, dx) in enumerate(peers):
+        if dy in VIA_IN and not dx:
+            halves[dy].wait_recv()
+            c = lax.rem(y + dy + NY, NY)
+            cpart[c, x] = cpart[c, x] + xslots[VIA_IN.index(dy)]
+            rs.append(
+                send(cpart.at[c, x], cslots.at[k], ys_sem.at[k], yr_sem.at[k], at_yx(dy, 0))
+            )
+
     for src, dst, small_src in ((dold_v, old_x, sold_v), (dmom_v, mom_x, smom_v)):
         dst[104:112, :] = jnp.zeros((8, 128), F32)
         for r in range(DENSE_ROWS):
@@ -205,21 +220,17 @@
         dst[108:109, :] = small_src[:, 0:128]
         dst[109:110, 0:112] = small_src[:, 128:240]
 
-    for copy in y_rs:
+    for copy in rs:
         copy.wait_recv()
-    for j in range(NX):
-        total = cpart[y, j]
-        for k in range(len(y_rs)):
-            total = total + cslots[k, j]
-        cmine[j] = total
-    mid = []
-    for k, (dx, dz) in enumerate(peers):
-        mid.append(
-            send(
-                cmine.at[lax.rem(x + dx, NX), lax.rem(z + dz + NZ, NZ)], cmid.at[k],
-                ms_sem.at[k], mr_sem.at[k], at_mid(dx, dz),
-            )
-        )
+    total = cpart[y, x]
+    for k, (dy, dx) in enumerate(peers):
+        if not (dx and dy in VIA_IN):
+            total = total + cslots[k]
+    cmine[...] = total
+    tiles = []
+    for k, offset in enumerate(FAR_FIRST):
+        src = cmine.at[lax.rem(z + offset + NZ, NZ)]
+        tiles.append(send(src, ctiles.at[k], ms_sem.at[k], mr_sem.at[k], at_z(offset)))
 
     for copy in z_rs:
         copy.wait_recv()
@@ -230,91 +241,131 @@
     new, moved = nesterov(old, mom_x[...], old - total / NZ)
     dfull[z] = new
     dmoved[...] = moved
-
-    z_ag = {}
-
-    def dense_send(k, offset):
-        z_ag[k] = send(dfull.at[z], dfull.at[z], zas_sem.at[k], zar_sem.at[k], at_z(offset))
-
+    z_ag = []
+
+    def dense_send(k):
+        z_ag.append(
+            send(dfull.at[z], dfull.at[z], zas_sem.at[k], zar_sem.at[k], at_z(FAR_FIRST[k]))
+        )
+
+    for k in NEAR:
+        dense_send(k)
+
+    for copy in tiles:
+        copy.wait_recv()
+    total = cmine[z]
+    for k in range(len(tiles)):
+        total = total + ctiles[k]
+    cfull[y, x, z] = total
+    tile = cfull.at[y, x, z]
+    tiles_back = []
     for k, offset in enumerate(FAR_FIRST):
-        if abs(offset) < 3:
-            dense_send(k, offset)
-
-    for copy in mid:
+        tiles_back.append(send(tile, tile, mas_sem.at[k], mar_sem.at[k], at_z(offset)))
+    for k in range(NZ - 1):
+        if k not in NEAR:
+            dense_send(k)
+    for copy in tiles_back:
         copy.wait_recv()
-    tile = cmine[x, z]
-    for k in range(len(peers)):
-        tile = tile + cmid[k]
-    ctile[...] = tile
-    cfull[y, x, z] = tile
-    mid_back = []
-    for k, (dx, dz) in enumerate(peers):
-        mid_back.append(
-            send(ctile, cfull.at[y, x, z], mas_sem.at[k], mar_sem.at[k], at_mid(dx, dz))
-        )
-    for k, offset in enumerate(FAR_FIRST):
-        if abs(offset) >= 3:
-            dense_send(k, offset)
-
-    for copy in mid_back:
-        copy.wait_recv()
-    y_ag = []
-    for k, offset in enumerate(FAR_FIRST):
-        y_ag.append(send(cfull.at[y], cfull.at[y], yas_sem.at[k], yar_sem.at[k], at_y(offset)))
-
-    stores = [pltpu.make_async_copy(dmoved, moved_out, store_sem.at[0])]
-    stores[0].start()
-    copy = pltpu.make_async_copy(cfull.at[y], cfull_out.at[y], store_sem.at[2])
-    copy.start()
-    stores.append(copy)
-    for k in range(len(FAR_FIRST)):
-        z_ag[k].wait_recv()
-    copy = pltpu.make_async_copy(dfull, full_out, store_sem.at[1])
-    copy.start()
-    stores.append(copy)
-    for k in (5, 6, 3, 4, 1, 2, 0):
-        y_ag[k].wait_recv()
-        c = lax.rem(y - FAR_FIRST[k] + NY, NY)
-        copy = pltpu.make_async_copy(cfull.at[c], cfull_out.at[c], store_sem.at[3 + k])
+    ag = {}
+
+    def pass_on(k, c, j, device):
+        block = cfull.at[c, j]
+        ag[peers[k]] = send(block, block, yas_sem.at[k], yar_sem.at[k], device)
+
+    for straight in (0, 1):
+        for k, (dy, dx) in enumerate(peers):
+            if dx == straight and not (dx and dy in VIA_OUT):
+                pass_on(k, y, x, at_yx(dy, dx))
+
+    stores = []
+
+    def store(src, dst):
+        copy = pltpu.make_async_copy(src, dst, store_sem.at[len(stores)])
         copy.start()
         stores.append(copy)
+
+    store(dmoved, moved_out)
+    store(cfull.at[y, x], cfull_out.at[y, x])
+    def arrive(dy, dx):
+        ag[dy, dx].wait_recv()
+        c, j = lax.rem(y - dy + NY, NY), lax.rem(x + dx, NX)
+        store(cfull.at[c, j], cfull_out.at[c, j])
+        return c
+
+    for dy in reversed(VIA_OUT):
+        c = arrive(dy, 0)
+        pass_on(peers.index((dy, 1)), c, x, at_yx(0, 1))
+    for dy, dx in reversed(peers):
+        if dy not in VIA_OUT:
+            arrive(dy, dx)
+    for copy in z_ag:
+        copy.wait_recv()
+    store(dfull, full_out)
+    for dy in reversed(VIA_OUT):
+        arrive(dy, 1)
     for copy in sends:
         copy.wait_send()
     for copy in stores:
         copy.wait()
 
 
-def finish_kernel(
-    full, moved, cfull, eo, ba, cm,
-    ai_o, ao_o, fi_o, fo_o, dm_o, sn_o, sm_o, en_o, cm_o,
-    ai_x, ao_x, fi_x, fo_x, sn_x,
-):
-    b_high, b_low = split_bf16(ba[...])
-    left = jnp.concatenate([b_high, b_low, b_high, b_low], axis=1)
-    for c in range(NY):
-        for j in range(2):
-            columns = slice(256 * c + 128 * j, 256 * c + 128 * j + 128)
-            coeff = cfull[c, j].reshape(RANK, 128) / NZ
-            coeff_moved = momentum_coef * cm[:, columns] + coeff
-            cm_o[:, columns] = coeff_moved
-            high, low = split_bf16(coeff + momentum_coef * coeff_moved)
-            right = jnp.concatenate([high, high, low, low], axis=0)
-            product = jnp.dot(left, right, preferred_element_type=F32)
-            en_o[:, columns] = eo[:, columns] - outer_rate * product
+def finish_kernel(*refs):
+    sources, targets = refs[:6], refs[6:15]
+    full, moved, cfull, eo, ba, cm = refs[15:21]
+    ai_o, ao_o, fi_o, fo_o, dm_o, sn_o, sm_o, en_o, cm_o = refs[21:30]
+    ai_x, ao_x, fi_x, fo_x, sn_x, load_sem, store_sem = refs[30:]
+
+    loads = []
+    for i, ref in enumerate((full, moved, cfull, eo, ba, cm)):
+        copy = pltpu.make_async_copy(sources[i], ref, load_sem.at[i])
+        copy.start()
+        loads.append(copy)
+    stores = []
+
+    def store(src, dst):
+        copy = pltpu.make_async_copy(src, dst, store_sem.at[len(stores)])
+        copy.start()
+        stores.append(copy)
+
+    loads[0].wait()
     unpack(full, (ai_x, ao_x, fi_x, fo_x))
     for which, (src, dst) in enumerate(((ai_x, ai_o), (ao_x, ao_o), (fi_x, fi_o), (fo_x, fo_o))):
         for t in range(TILES[which]):
             size = min(128, WIDTHS[which] - 128 * t)
             dst[:, 128 * t : 128 * t + size] = src[t, :, 0:size]
+        store(dst, targets[which])
+    loads[1].wait()
     for r in range(DENSE_ROWS):
         dm_o[:, 128 * r : 128 * r + 128] = moved[r : r + 1, :]
+    store(dm_o, targets[4])
     sm_o[:, 0:128] = moved[108:109, :]
     sm_o[:, 128:240] = moved[109:110, 0:112]
+    store(sm_o, targets[6])
     for owner in range(NZ):
         sn_x[:, 240 * owner : 240 * owner + 128] = full[owner, 108:109, :]
         sn_x[:, 240 * owner + 128 : 240 * owner + 240] = full[owner, 109:110, 0:112]
     for r in range(15):
         sn_o[r : r + 1, :] = sn_x[:, 128 * r : 128 * r + 128]
+    store(sn_o, targets[5])
+    for copy in loads[2:]:
+        copy.wait()
+    b_high, b_low = split_bf16(ba[...])
+    left = jnp.concatenate([b_high, b_low, b_high, b_low], axis=1)
+    for c in range(NY):
+        columns = slice(256 * c, 256 * c + 256)
+        coeff = jnp.concatenate([cfull[c, j].reshape(RANK, 128) for j in range(2)], axis=1) / NZ
+        coeff_moved = momentum_coef * cm[:, columns] + coeff
+        cm_o[:, columns] = coeff_moved
+        high, low = split_bf16(coeff + momentum_coef * coeff_moved)
+        right = jnp.concatenate([high, high, low, low], axis=0)
+        product = jnp.dot(left, right, preferred_element_type=F32)
+        en_o[:, columns] = eo[:, columns] - outer_rate * product
+        if c % 2:
+            columns = slice(256 * c - 256, 256 * c + 256)
+            store(cm_o.at[:, columns], targets[8].at[:, columns])
+            store(en_o.at[:, columns], targets[7].at[:, columns])
+    for copy in stores:
+        copy.wait()
 
 
 def shards(
@@ -333,7 +384,6 @@
     coeff_momentum,
 ):
     any_spec = pl.BlockSpec(memory_space=pl.ANY)
-    vmem_spec = pl.BlockSpec(memory_space=pltpu.VMEM)
     dma = pltpu.SemaphoreType.DMA
     tile_scratch = [
         pltpu.VMEM((TILES[i], HEIGHTS[i], 128), F32) for i in range(4)
@@ -362,38 +412,37 @@
             pltpu.VMEM((NZ, ROWS, 128), F32),
             pltpu.VMEM((ROWS, 128), F32),
             pltpu.VMEM((NY, NX, NZ, 8, 128), F32),
-            pltpu.VMEM((NY - 1, NX, NZ, 8, 128), F32),
-            pltpu.VMEM((NX, NZ, 8, 128), F32),
-            pltpu.VMEM((NX * NZ - 1, 8, 128), F32),
-            pltpu.VMEM((8, 128), F32),
+            pltpu.VMEM((NY * NX - 1, NZ, 8, 128), F32),
+            pltpu.VMEM((max(1, len(VIA_IN)), NZ, 8, 128), F32),
+            pltpu.VMEM((NZ, 8, 128), F32),
+            pltpu.VMEM((NZ - 1, 8, 128), F32),
             pltpu.VMEM((NY, NX, NZ, 8, 128), F32),
             dma((len(operands),)),
-            dma((10,)),
+            dma((NY * NX + 2,)),
         ]
-        + [dma((7,))] * 8
-        + [dma((NX * NZ - 1,))] * 4,
+        + [dma((NZ - 1,))] * 4
+        + [dma((NY * NX - 1,))] * 4
+        + [dma((NZ - 1,))] * 4,
         compiler_params=pltpu.CompilerParams(collective_id=0, has_side_effects=True),
         name="exchange",
     )(*operands)
 
+    finish_args = (full, moved, cfull, embed_old, basis, coeff_momentum)
+    results = (
+        (48, 576), (48, 192), (48, 768), (192, 192), (1, 13824), (15, 128), (1, 240),
+        (48, 2048), (RANK, 2048),
+    )
     outs = pl.pallas_call(
         finish_kernel,
-        out_shape=(
-            jax.ShapeDtypeStruct((48, 576), F32),
-            jax.ShapeDtypeStruct((48, 192), F32),
-            jax.ShapeDtypeStruct((48, 768), F32),
-            jax.ShapeDtypeStruct((192, 192), F32),
-            jax.ShapeDtypeStruct((1, 13824), F32),
-            jax.ShapeDtypeStruct((15, 128), F32),
-            jax.ShapeDtypeStruct((1, 240), F32),
-            jax.ShapeDtypeStruct((48, 2048), F32),
-            jax.ShapeDtypeStruct((RANK, 2048), F32),
-        ),
-        in_specs=[vmem_spec] * 6,
-        out_specs=[vmem_spec] * 9,
-        scratch_shapes=tile_scratch + [pltpu.VMEM((1, 1920), F32)],
+        out_shape=[jax.ShapeDtypeStruct(shape, F32) for shape in results],
+        in_specs=[any_spec] * len(finish_args),
+        out_specs=[any_spec] * len(results),
+        scratch_shapes=[pltpu.VMEM(a.shape, F32) for a in finish_args]
+        + [pltpu.VMEM(shape, F32) for shape in results]
+        + tile_scratch
+        + [pltpu.VMEM((1, 1920), F32), dma((len(finish_args),)), dma((15,))],
         name="finish",
-    )(full, moved, cfull, embed_old, basis, coeff_momentum)
+    )(*finish_args)
     return (
         outs[0], outs[1], outs[2], outs[3], outs[4],
         outs[5].reshape(-1), outs[6].reshape(-1), outs[7], outs[8],

time: 55.4 us -> 53 us (0.957)
  Pallas kernels: 54.1 us -> 51.7 us
    pallas_call x1, Pallas kernels: 51.2 us -> 48.9 us  [shards(): pl.pallas_call(comm_kernel, out_shape=(jax.ShapeDtypeStruct((NZ, ROWS, 12...]
where the time goes in v3:
time: 53 us; the launch traced here: 52.3 us
  Pallas kernels  51.7 us (98%)
  between operations  0.65 us (1%)
    pallas_call x1, Pallas kernels, shards(): pl.pallas_call(comm_kernel, out_shape=(jax.ShapeDtypeStruct((NZ, ROWS, 12...  48.9 us
    pallas_call x1, Pallas kernels, shards(): pl.pallas_call(finish_kernel, out_shape=[jax.ShapeDtypeStruct(shape, F32)...  2.8 us

profile of v3, /device:TPU:6, one launch (start us, length us, event | category | flops | bytes accessed | tf_op | source)
XLA Modules:
  0.0 52.3 jit_solution(10784144978544366012)
XLA Ops:
  0.6 48.9 %exchange.1 = (f32[8,112,128]{2,1,0:T(8,128)}, f32[112,128]{1,0:T(8,128)}, f32[8,2,8,8,128]{4,3,2,1,0:T(8,128)}) custom-call(bf16[1,48,576]{2,1,0:T(8,128)(2,1)} %refs_0_.1, bf16[1,48,192]{2,1,0:T(8,128)(2,1)} %refs_1_.1, bf16[1,48,768]{2,1,0:T(8,128)(2,1)} %refs_2_.1, bf16[1,192,192]{2,1,0:T(8,128)(2,1)} %refs_3_.2, bf16[1,1920]{1,0:T(2,128)(2,1)} %refs_4_.2, ...), custom_call_target="tpu_custom_call" | custom-call | tf_op jit(solution)/shard_map/exchange/pallas_call | solution.py:396
  49.5 2.8 %finish.1 = (f32[48,576]{1,0:T(8,128)}, f32[48,192]{1,0:T(8,128)}, f32[48,768]{1,0:T(8,128)}, f32[192,192]{1,0:T(8,128)}, f32[1,13824]{1,0:T(1,128)}, /*index=5*...) custom-call(f32[8,112,128]{2,1,0:T(8,128)} %get-tuple-element.21.refs_0_, ...), custom_call_target="tpu_custom_call" | custom-call | tf_op jit(solution)/shard_map/finish/pallas_call | solution.py:435
